TPU v7x, 32 devices: a whole 2x2x4 slice. The times are simulated.
32 devices in a mesh: leaf: 8 (over z, y), rows: 4 (over x, core).
Axes of the slice: x: 2, y: 2, z: 4, core: 2. Of those that a mesh axis runs over, the one named last changes fastest.
Arguments:
- factor_zero: bfloat16 [4096, 4096], P('leaf', 'rows'), may hold values from -1 to 3, as said below
- factor_one: bfloat16 [8192, 4096], P('leaf', 'rows'), may hold values from -1 to 3, as said below
- factor_two: bfloat16 [16384, 4096], P('leaf', 'rows'), may hold values from -1 to 3, as said below
- factor_three: bfloat16 [32768, 4096], P('leaf', 'rows'), may hold values from -1 to 3, as said below
- coupling_one: bfloat16 [8192, 1, 4096], P('leaf', None, 'rows'), may hold values from -0.046875 to 0.046875
- coupling_two: bfloat16 [16384, 2, 4096], P('leaf', None, 'rows'), may hold values from -0.046875 to 0.046875
- coupling_three: bfloat16 [32768, 3, 4096], P('leaf', None, 'rows'), may hold values from -0.046875 to 0.046875
- noise_zero: bfloat16 [4096, 128], P('leaf'), may hold values from -6 to 6
- noise_one: bfloat16 [8192, 128], P('leaf'), may hold values from -6 to 6
- noise_two: bfloat16 [16384, 128], P('leaf'), may hold values from -6 to 6
- noise_three: bfloat16 [32768, 128], P('leaf'), may hold values from -6 to 6
- tail_index: int32 [16], replicated, may hold values from 0 to 127
Outputs:
- grad_zero: float32 [4096, 128], P('leaf')
- grad_one: float32 [8192, 128], P('leaf')
- grad_two: float32 [16384, 128], P('leaf')
- grad_three: float32 [32768, 128], P('leaf')
- tail_loss: float32 [], replicated
Inputs may be any that keep to these rules, and one draw needn't show every extreme that they name: `factor_zero`: each 4096 x 4096 node block is lower triangular with a positive diagonal. `factor_one`: each 4096 x 4096 node block is lower triangular with a positive diagonal. `factor_two`: each 4096 x 4096 node block is lower triangular with a positive diagonal. `factor_three`: each 4096 x 4096 node block is lower triangular with a positive diagonal.
All inputs are finite; a program needn't handle non-finite values.
Results may differ from a plain program's by a relative error of at most 0.008.
Values sent between devices are 32-bit elements; how exact they have to be, the bound alone decides.
No kernel may reach another device: no remote copies, remote signals or barrier semaphores. Data moves between devices by JAX's collectives and lax.ppermute only.
A program may use at most 192 MiB of HBM per device.

v0:
```python
import jax
import jax.numpy as jnp
from jax import lax
from jax.sharding import PartitionSpec as P

LEVELS = 4


tail_level = 0.5


def swapped(x, axis, apart):
    return lax.ppermute(x, axis, [(i, i ^ 1 << apart) for i in range(lax.axis_size(axis))])


def halve_bits(partial_value, bit_count, leaf_index):
    for position in range(bit_count):
        half_rows = partial_value.shape[0] // 2
        upper_bit = leaf_index >> position & 1
        kept_half = lax.dynamic_slice_in_dim(partial_value, upper_bit * half_rows, half_rows, 0)
        sent_half = lax.dynamic_slice_in_dim(
            partial_value, (1 - upper_bit) * half_rows, half_rows, 0
        )
        partial_value = kept_half + swapped(sent_half, "leaf", position)
    return partial_value


def double_bits(partial_value, bit_count, leaf_index):
    for position in reversed(range(bit_count)):
        partner = swapped(partial_value, "leaf", position)
        upper_bit = leaf_index >> position & 1
        partial_value = jnp.where(
            upper_bit == 1,
            jnp.concatenate([partner, partial_value], axis=0),
            jnp.concatenate([partial_value, partner], axis=0),
        )
    return partial_value


def group_sum(partial_value, group_bits, leaf_index):
    halved_bits = min(2, group_bits)
    partial_value = halve_bits(partial_value, halved_bits, leaf_index)
    for position in range(halved_bits, group_bits):
        partial_value = partial_value + swapped(partial_value, "leaf", position)
    return double_bits(partial_value, halved_bits, leaf_index)


def on_device(
    factor_zero,
    factor_one,
    factor_two,
    factor_three,
    coupling_one,
    coupling_two,
    coupling_three,
    noise_zero,
    noise_one,
    noise_two,
    noise_three,
    tail_index,
):
    factors = [factor_zero, factor_one, factor_two, factor_three]
    couplings = [None, coupling_one, coupling_two, coupling_three]
    noises = [noise_zero, noise_one, noise_two, noise_three]
    leaf_bits = lax.axis_size("leaf").bit_length() - 1
    leaf_index = lax.axis_index("leaf")
    full_width = factor_zero.shape[1] * lax.axis_size("rows")
    scenario_count = noise_zero.shape[1]
    columns = jnp.arange(scenario_count, dtype=jnp.int32)
    counts = jnp.sum((tail_index[:, None] == columns[None, :]).astype(jnp.float32), axis=0)
    weights = 1.0 + counts
    contract_rows = (((0,), (0,)), ((), ()))
    rounded = []
    cotangents = []
    loss_sum = jnp.float32(0.0)
    for tree_level in range(LEVELS):
        group_bits = leaf_bits - tree_level
        right_side = noises[tree_level].astype(jnp.float32)
        if tree_level > 0:
            coupling = couplings[tree_level]
            flat_coupling = coupling.reshape(
                coupling.shape[0], coupling.shape[1] * coupling.shape[2]
            )
            stacked = jnp.concatenate(rounded, axis=0)
            ancestor_terms = jnp.dot(flat_coupling, stacked, preferred_element_type=jnp.float32)
            right_side = right_side - lax.psum(ancestor_terms, "rows")
        right_round = right_side.astype(jnp.bfloat16)
        partial_sample = lax.dot_general(
            factors[tree_level], right_round, contract_rows, preferred_element_type=jnp.float32
        )
        sample = group_sum(partial_sample, group_bits, leaf_index)
        rounded.append(sample.astype(jnp.bfloat16))
        shifted = sample - tail_level
        cotangents.append(weights[None, :] * jax.nn.sigmoid(shifted))
        piece_rows = sample.shape[0] >> group_bits
        member = leaf_index & (1 << group_bits) - 1
        own_rows = lax.dynamic_slice_in_dim(shifted, member * piece_rows, piece_rows, 0)
        loss_sum = loss_sum + jnp.sum(weights[None, :] * jax.nn.softplus(own_rows))
    loss_total = lax.psum(loss_sum, ("leaf", "rows"))
    tail_loss = loss_total / jnp.float32(
        (2**LEVELS - 1) * full_width * (scenario_count + tail_index.shape[0])
    )
    pending = [jnp.zeros_like(cotangents[0]) for tree_level in range(LEVELS - 1)]
    gradients = [None] * LEVELS
    for tree_level in reversed(range(LEVELS)):
        group_bits = leaf_bits - tree_level
        if tree_level == LEVELS - 1:
            adjoint = cotangents[tree_level]
        else:
            adjoint = cotangents[tree_level] - group_sum(
                pending[tree_level], group_bits, leaf_index
            )
        adjoint_round = adjoint.astype(jnp.bfloat16)
        solved_terms = jnp.dot(
            factors[tree_level], adjoint_round, preferred_element_type=jnp.float32
        )
        solved_exact = lax.psum(solved_terms, "rows")
        gradients[tree_level] = solved_exact
        if tree_level > 0:
            solved = solved_exact.astype(jnp.bfloat16)
            upward = lax.dot_general(
                couplings[tree_level], solved, contract_rows, preferred_element_type=jnp.float32
            )
            for ancestor in range(tree_level):
                pending[ancestor] = pending[ancestor] + upward[ancestor]
    return (gradients[0], gradients[1], gradients[2], gradients[3], tail_loss)


def solution(mesh):
    in_specs = (
        P("leaf", "rows"),
        P("leaf", "rows"),
        P("leaf", "rows"),
        P("leaf", "rows"),
        P("leaf", None, "rows"),
        P("leaf", None, "rows"),
        P("leaf", None, "rows"),
        P("leaf", None),
        P("leaf", None),
        P("leaf", None),
        P("leaf", None),
        P(),
    )
    out_specs = (P("leaf", None), P("leaf", None), P("leaf", None), P("leaf", None), P())
    return jax.shard_map(
        on_device, mesh=mesh, in_specs=in_specs, out_specs=out_specs, check_vma=False
    )
```

profile of v0, /device:TPU:0, one launch (start us, length us, event | category | flops | bytes accessed | tf_op | source)
XLA Modules:
  0.0 573.5 jit_solution(12728967420345723945)
XLA Ops:
  7.2 1.8 fusion.81
  9.1 3.0 collective-permute-start
  12.1 6.3 %collective-permute-done = f32[512,128]{1,0:T(8,128)S(1)} collective-permute-done((f32[512,128]{1,0:T(8,128)S(1)}, f32[512,128]{1,0:T(8,128)S(1)}, u32[]{:S(2)}, u32[]{:S(2)}) %collective-permute-start) | collective-permute-done | bytes 262176 | tf_op jit(solution)/shard_map/ppermute | solution.py:13
  18.5 1.9 collective-permute-start.1
  20.4 3.2 collective-permute-done.1
  23.6 2.7 collective-permute-start.2
  26.3 4.7 collective-permute-done.2
  31.7 4.3 collective-permute-done.3
  37.9 4.6 collective-permute-done.4
  42.6 3.3 fusion.9
  46.1 34.3 %all-reduce.8.cloned.1.call-done = f32[1024,128]{0,1:T(8,128)} async-done(((f32[1024,128]{0,1:T(8,128)}), f32[1024,128]{0,1:T(8,128)}) %all-reduce.8.cloned.1.call-update) | async-done | bytes 524304 | tf_op jit(solution)/shard_map/psum | solution.py:86
  80.4 2.0 fusion.50
  83.9 5.4 collective-permute-done.5
  91.2 3.7 collective-permute-done.6
  94.9 1.8 collective-permute-start.7
  96.7 3.2 collective-permute-done.7
  101.8 10.1 %copy.67 = bf16[256,8,2,1024]{3,1,2,0:T(8,128)(2,1)} copy(bf16[256,8,2,1024]{3,2,1,0:T(2,128)(2,1)} %bitcast.79) | data formatting | bytes 16777216
  112.0 7.3 %convolution_bitcast_fusion.2 = f32[2048,128]{0,1:T(8,128)} fusion(bf16[2048,2048]{1,0:T(8,128)(2,1)} %bitcast.78, bf16[1024,128]{1,0:T(8,128)(2,1)S(1)} %fusion.44, bf16[1024,128]{1,0:T(8,128)(2,1)S(1)} %fusion.45), kind=kOutput, calls=%fused_computation.4 | convolution fusion | flops 1074790400 | bytes 9961472 | tf_op jit(solution)/shard_map/dot_general | solution.py:85
  120.8 33.8 %all-reduce.10.cloned.1.call-done = f32[2048,128]{0,1:T(8,128)} async-done(((f32[2048,128]{0,1:T(8,128)}), f32[2048,128]{0,1:T(8,128)}) %all-reduce.10.cloned.1.call-update) | async-done | bytes 1048592 | tf_op jit(solution)/shard_map/psum | solution.py:86
  154.6 4.2 fusion.26
  160.5 6.4 %collective-permute-done.9 = f32[512,128]{1,0:T(8,128)S(1)} collective-permute-done((f32[512,128]{1,0:T(8,128)S(1)}, f32[512,128]{1,0:T(8,128)S(1)}, u32[]{:S(2)}, u32[]{:S(2)}) %collective-permute-start.9) | collective-permute-done | bytes 262176 | tf_op jit(solution)/shard_map/ppermute | solution.py:13
  168.2 33.4 %copy.51 = bf16[4096,3,1024]{0,2,1:T(8,128)(2,1)} copy(bf16[4096,3,1024]{2,0,1:T(8,128)(2,1)} %param.18) | data formatting | bytes 50331648 | tf_op args[6]
  202.6 12.9 %convolution_bitcast_fusion.1 = f32[4096,128]{0,1:T(8,128)} fusion(bf16[4096,3072]{0,1:T(8,128)(2,1)} %bitcast.77, bf16[1024,128]{1,0:T(8,128)(2,1)S(1)} %fusion.42, bf16[1024,128]{1,0:T(8,128)(2,1)S(1)} %fusion.44, bf16[1024,128]{1,0:T(8,128)(2,1)S(1)} %fusion.45), kind=kOutput, calls=%fused_computation.3 | convolution fusion | flops 3223584768 | bytes 28049408 | tf_op jit(solution)/shard_map/dot_general | solution.py:85
  217.2 49.7 %all-reduce.12.cloned.1.call-done = f32[4096,128]{0,1:T(8,128)} async-done(((f32[4096,128]{0,1:T(8,128)}), f32[4096,128]{0,1:T(8,128)}) %all-reduce.12.cloned.1.call-update) | async-done | bytes 2097168 | tf_op jit(solution)/shard_map/psum | solution.py:86
  266.9 7.4 %fusion.28 = (f32[]{:T(128)}, f32[1024,128]{1,0:T(8,128)S(1)}) fusion(f32[128]{0:T(128)S(1)} %broadcast_add_fusion, bf16[4096,1024]{1,0:T(8,128)(2,1)} %param.15, f32[4096,128]{0,1:T(8,128)} %all-reduce.12.cloned.1.call-done, bf16[4096,128]{0,1:T(8,128)(2,1)S(1)} %copy.44), kind=kOutput, calls=%fused_computation.32 | convolution fusion | flops 1076494336 | bytes 12059140 | tf_op jit(solution)/shard_map/dot_general | solution.py:88
  274.3 7.6 %convolution_bitcast_fusion = f32[4096,128]{0,1:T(8,128)} fusion(bf16[4096,1024]{1,0:T(8,128)(2,1)} %param.15, f32[1024,128]{1,0:T(8,128)S(1)} %get-tuple-element.21, f32[128]{0:T(128)S(1)} %broadcast_add_fusion), kind=kOutput, calls=%fused_computation.2 | convolution fusion | flops 1074397184 | bytes 11010560 | tf_op jit(solution)/shard_map/dot_general | solution.py:114
  282.3 51.3 %all-reduce.14.cloned.1.call-done = f32[4096,128]{0,1:T(8,128)} async-done(((f32[4096,128]{0,1:T(8,128)}), f32[4096,128]{0,1:T(8,128)}) %all-reduce.14.cloned.1.call-update) | async-done | bytes 2097168 | tf_op jit(solution)/shard_map/psum | solution.py:117
  333.6 16.0 %convolution_bitcast_fusion.4 = f32[3,1024,128]{2,1,0:T(8,128)} fusion(bf16[4096,3,1024]{2,0,1:T(8,128)(2,1)} %param.18, f32[4096,128]{0,1:T(8,128)} %all-reduce.14.cloned.1.call-done), kind=kOutput, calls=%fused_computation.12 | convolution fusion | flops 3221749760 | bytes 28835840 | tf_op jit(solution)/shard_map/dot_general | solution.py:121
  352.4 6.5 %collective-permute-done.11 = f32[512,128]{1,0:T(8,128)S(1)} collective-permute-done((f32[512,128]{1,0:T(8,128)S(1)}, f32[512,128]{1,0:T(8,128)S(1)}, u32[]{:S(2)}, u32[]{:S(2)}) %collective-permute-start.11) | collective-permute-done | bytes 262176 | tf_op jit(solution)/shard_map/ppermute | solution.py:13
  360.4 5.6 collective-permute-done.12
  366.1 4.9 convolution_bitcast_fusion.3
  371.0 36.6 %all-reduce.16.cloned.1.call-done = f32[2048,128]{0,1:T(8,128)} async-done(((f32[2048,128]{0,1:T(8,128)}), f32[2048,128]{0,1:T(8,128)}) %all-reduce.16.cloned.1.call-update) | async-done | bytes 1048592 | tf_op jit(solution)/shard_map/psum | solution.py:117
  407.6 7.6 %fusion.6 = f32[2,1024,128]{2,1,0:T(8,128)S(1)} fusion(bf16[2048,2,1024]{2,1,0:T(2,128)(2,1)} %param.17, f32[2048,128]{0,1:T(8,128)} %all-reduce.16.cloned.1.call-done), kind=kOutput, calls=%fused_computation.13 | convolution fusion | flops 1074003968 | bytes 10485760 | tf_op jit(solution)/shard_map/dot_general | solution.py:121
  418.3 6.4 %collective-permute-done.13 = f32[512,128]{1,0:T(8,128)S(1)} collective-permute-done((f32[512,128]{1,0:T(8,128)S(1)}, f32[512,128]{1,0:T(8,128)S(1)}, u32[]{:S(2)}, u32[]{:S(2)}) %collective-permute-start.13) | collective-permute-done | bytes 262176 | tf_op jit(solution)/shard_map/ppermute | solution.py:13
  426.0 3.7 collective-permute-done.14
  431.1 3.7 collective-permute-done.15
  436.1 5.1 collective-permute-done.16
  443.3 33.5 %all-reduce.18.cloned.1.call-done = f32[1024,128]{0,1:T(8,128)} async-done(((f32[1024,128]{0,1:T(8,128)}), f32[1024,128]{0,1:T(8,128)}) %all-reduce.18.cloned.1.call-update) | async-done | bytes 524304 | tf_op jit(solution)/shard_map/psum | solution.py:117
  476.8 2.9 fusion.15
  481.3 5.4 collective-permute-done.17
  488.5 3.2 collective-permute-done.18
  491.7 3.3 collective-permute-start.19
  495.0 4.4 collective-permute-done.19
  501.4 3.1 collective-permute-done.20
  511.8 2.9 convolution_bitcast_fusion.6
  516.8 39.7 %psum.63 = f32[]{:T(128)} all-reduce(f32[]{:T(128)S(6)} %add.189), channel_id=1, replica_groups=mesh['leaf'=8,'rows'=4] {'leaf','rows'}, use_global_device_ids=true, to_apply=%region_12.13 | all-reduce | flops 1 | bytes 8 | tf_op jit(solution)/shard_map/psum | solution.py:99
  557.2 2.9 copy.60
  560.1 2.6 copy.59
  (104 shorter events, 44.2 us)
Async XLA Ops:
  7.2 73.2 %copy-start = (bf16[1024,1024]{1,0:T(8,128)(2,1)S(1)}, bf16[1024,1024]{1,0:T(8,128)(2,1)}, u32[]{:S(2)}) copy-start(bf16[1024,1024]{1,0:T(8,128)(2,1)} %param.13) | copy-start | bytes 6291460
  7.2 73.2 %all-reduce.8.cloned.1.call-start = ((), (), s32[]{:S(2)}) async-start(), calls=%async_computation | async-start | bytes 1048576 | tf_op jit(solution)/shard_map/psum | solution.py:86
  9.1 9.3 %collective-permute-start = (f32[512,128]{1,0:T(8,128)S(1)}, f32[512,128]{1,0:T(8,128)S(1)}, u32[]{:S(2)}, u32[]{:S(2)}) collective-permute-start(f32[512,128]{1,0:T(8,128)S(1)} %constant_dynamic-slice_fusion.5), channel_id=1, source_target_pairs={{0,4},{4,0},{8,12},{12,8},{16,20},{20,16},{24,28},{28,24},{1,5},{5... | collective-permute-start | bytes 786440 | tf_op jit(solution)/shard_map/ppermute | solution.py:13
  18.5 5.0 collective-permute-start.1
  23.6 7.4 %collective-permute-start.2 = (f32[256,128]{1,0:T(8,128)S(1)}, f32[256,128]{1,0:T(8,128)S(1)}, u32[]{:S(2)}, u32[]{:S(2)}) collective-permute-start(f32[256,128]{1,0:T(8,128)S(1)} %dynamic-slice_add_fusion.5), channel_id=1, source_target_pairs={{0,16},{4,20},{8,24},{12,28},{16,0},{20,4},{24,8},{28,12},{1,17},{... | collective-permute-start | bytes 393224 | tf_op jit(solution)/shard_map/ppermute | solution.py:13
  31.0 5.0 collective-permute-start.3
  36.1 6.4 %collective-permute-start.4 = (f32[512,128]{1,0:T(8,128)S(1)}, f32[512,128]{1,0:T(8,128)S(1)}, u32[]{:S(2)}, u32[]{:S(2)}) collective-permute-start(f32[512,128]{1,0:T(8,128)S(1)} %maximum_select_fusion.6), channel_id=1, source_target_pairs={{0,4},{4,0},{8,12},{12,8},{16,20},{20,16},{24,28},{28,24},{1,5},{5... | collective-permute-start | bytes 786440 | tf_op jit(solution)/shard_map/ppermute | solution.py:13
  37.9 8.0 %copy-start.10 = (bf16[1024,128]{1,0:T(8,128)(2,1)S(1)}, bf16[1024,128]{1,0:T(8,128)(2,1)}, u32[]{:S(2)}) copy-start(bf16[1024,128]{1,0:T(8,128)(2,1)} %param.20) | copy-start | bytes 786436
  42.5 3.4 copy-start.7
  45.9 108.8 %all-reduce.10.cloned.1.call-start = ((), (), s32[]{:S(2)}) async-start(), calls=%async_computation.1 | async-start | bytes 2097152 | tf_op jit(solution)/shard_map/psum | solution.py:86
  82.4 6.9 %collective-permute-start.5 = (f32[512,128]{1,0:T(8,128)S(1)}, f32[512,128]{1,0:T(8,128)S(1)}, u32[]{:S(2)}, u32[]{:S(2)}) collective-permute-start(f32[512,128]{1,0:T(8,128)S(1)} %dynamic-slice_bitcast_fusion.3), channel_id=1, source_target_pairs={{0,4},{4,0},{8,12},{12,8},{16,20},{20,16},{24,28},{28,24},{1,5},{5... | collective-permute-start | bytes 786440 | tf_op jit(solution)/shard_map/ppermute | solution.py:13
  89.4 5.5 collective-permute-start.6
  94.9 5.0 collective-permute-start.7
  100.0 12.0 %copy-start.1 = (f32[512,128]{1,0:T(8,128)}, f32[512,128]{1,0:T(8,128)S(1)}, u32[]{:S(2)}) copy-start(f32[512,128]{1,0:T(8,128)S(1)} %maximum_select_fusion.7) | copy-start | bytes 786436
  100.0 12.0 %collective-permute-start.8 = (f32[512,128]{1,0:T(8,128)S(1)}, f32[512,128]{1,0:T(8,128)S(1)}, u32[]{:S(2)}, u32[]{:S(2)}) collective-permute-start(f32[512,128]{1,0:T(8,128)S(1)} %maximum_select_fusion.7), channel_id=1, source_target_pairs={{0,4},{4,0},{8,12},{12,8},{16,20},{20,16},{24,28},{28,24},{1,5},{5... | collective-permute-start | bytes 786440 | tf_op jit(solution)/shard_map/ppermute | solution.py:13
  111.9 7.4 %copy-start.8 = (f32[512,128]{1,0:T(8,128)}, f32[512,128]{1,0:T(8,128)S(1)}, u32[]{:S(2)}) copy-start(f32[512,128]{1,0:T(8,128)S(1)} %collective-permute-done.8) | copy-start | bytes 786436
  119.3 147.6 %all-reduce.12.cloned.1.call-start = ((), (), s32[]{:S(2)}) async-start(), calls=%async_computation.2 | async-start | bytes 4194304 | tf_op jit(solution)/shard_map/psum | solution.py:86
  158.9 7.9 %collective-permute-start.9 = (f32[512,128]{1,0:T(8,128)S(1)}, f32[512,128]{1,0:T(8,128)S(1)}, u32[]{:S(2)}, u32[]{:S(2)}) collective-permute-start(f32[512,128]{1,0:T(8,128)S(1)} %dynamic-slice_bitcast_fusion.2), channel_id=1, source_target_pairs={{0,4},{4,0},{8,12},{12,8},{16,20},{20,16},{24,28},{28,24},{1,5},{5... | collective-permute-start | bytes 786440 | tf_op jit(solution)/shard_map/ppermute | solution.py:13
  166.9 34.7 %copy-start.3 = (f32[512,128]{1,0:T(8,128)}, f32[512,128]{1,0:T(8,128)S(1)}, u32[]{:S(2)}) copy-start(f32[512,128]{1,0:T(8,128)S(1)} %bitcast_add_fusion.2) | copy-start | bytes 786436
  166.9 34.7 %collective-permute-start.10 = (f32[512,128]{1,0:T(8,128)S(1)}, f32[512,128]{1,0:T(8,128)}, u32[]{:S(2)}, u32[]{:S(2)}) collective-permute-start(f32[512,128]{1,0:T(8,128)S(1)} %bitcast_add_fusion.2), channel_id=1, source_target_pairs={{0,4},{4,0},{8,12},{12,8},{16,20},{20,16},{24,28},{28,24},{1,5},{5... | collective-permute-start | bytes 786440 | tf_op jit(solution)/shard_map/ppermute | solution.py:13
  215.6 1.6 copy-start.11
  215.6 118.0 %all-reduce.14.cloned.1.call-start = ((), (), s32[]{:S(2)}) async-start(), calls=%async_computation.3 | async-start | bytes 4194304 | tf_op jit(solution)/shard_map/psum | solution.py:117
  282.0 125.6 %all-reduce.16.cloned.1.call-start = ((), (), s32[]{:S(2)}) async-start(), calls=%async_computation.4 | async-start | bytes 2097152 | tf_op jit(solution)/shard_map/psum | solution.py:117
  349.7 16.4 %copy-start.4 = (f32[512,128]{1,0:T(8,128)S(1)}, f32[512,128]{1,0:T(8,128)}, u32[]{:S(2)}) copy-start(f32[512,128]{1,0:T(8,128)} %copy-done.3) | copy-start | bytes 786436
  350.8 8.0 %collective-permute-start.11 = (f32[512,128]{1,0:T(8,128)S(1)}, f32[512,128]{1,0:T(8,128)S(1)}, u32[]{:S(2)}, u32[]{:S(2)}) collective-permute-start(f32[512,128]{1,0:T(8,128)S(1)} %dynamic-slice_bitcast_fusion.1), channel_id=1, source_target_pairs={{0,4},{4,0},{8,12},{12,8},{16,20},{20,16},{24,28},{28,24},{1,5},{5... | collective-permute-start | bytes 786440 | tf_op jit(solution)/shard_map/ppermute | solution.py:13
  358.9 7.2 %collective-permute-start.12 = (f32[512,128]{1,0:T(8,128)S(1)}, f32[512,128]{1,0:T(8,128)S(1)}, u32[]{:S(2)}, u32[]{:S(2)}) collective-permute-start(f32[512,128]{1,0:T(8,128)S(1)} %bitcast_add_fusion.1), channel_id=1, source_target_pairs={{0,4},{4,0},{8,12},{12,8},{16,20},{20,16},{24,28},{28,24},{1,5},{5... | collective-permute-start | bytes 786440 | tf_op jit(solution)/shard_map/ppermute | solution.py:13
  371.0 105.8 %all-reduce.18.cloned.1.call-start = ((), (), s32[]{:S(2)}) async-start(), calls=%async_computation.5 | async-start | bytes 1048576 | tf_op jit(solution)/shard_map/psum | solution.py:117
  415.1 14.6 %copy-start.6 = (f32[2,1024,128]{2,1,0:T(8,128)}, f32[2,1024,128]{2,1,0:T(8,128)S(1)}, u32[]{:S(2)}) copy-start(f32[2,1024,128]{2,1,0:T(8,128)S(1)} %fusion.6) | copy-start | bytes 3145732
  415.2 26.1 %copy-start.2 = (f32[512,128]{1,0:T(8,128)S(1)}, f32[512,128]{1,0:T(8,128)}, u32[]{:S(2)}) copy-start(f32[512,128]{1,0:T(8,128)} %copy-done.1) | copy-start | bytes 786436
  415.2 26.1 %copy-start.9 = (f32[512,128]{1,0:T(8,128)S(1)}, f32[512,128]{1,0:T(8,128)}, u32[]{:S(2)}) copy-start(f32[512,128]{1,0:T(8,128)} %copy-done.8) | copy-start | bytes 786436
  416.7 7.9 %collective-permute-start.13 = (f32[512,128]{1,0:T(8,128)S(1)}, f32[512,128]{1,0:T(8,128)S(1)}, u32[]{:S(2)}, u32[]{:S(2)}) collective-permute-start(f32[512,128]{1,0:T(8,128)S(1)} %dynamic-slice_bitcast_fusion), channel_id=1, source_target_pairs={{0,4},{4,0},{8,12},{12,8},{16,20},{20,16},{24,28},{28,24},{1,5},{5... | collective-permute-start | bytes 786440 | tf_op jit(solution)/shard_map/ppermute | solution.py:13
  424.7 5.0 collective-permute-start.14
  429.7 5.0 collective-permute-start.15
  434.8 6.4 %collective-permute-start.16 = (f32[512,128]{1,0:T(8,128)S(1)}, f32[512,128]{1,0:T(8,128)S(1)}, u32[]{:S(2)}, u32[]{:S(2)}) collective-permute-start(f32[512,128]{1,0:T(8,128)S(1)} %maximum_select_fusion.8), channel_id=1, source_target_pairs={{0,4},{4,0},{8,12},{12,8},{16,20},{20,16},{24,28},{28,24},{1,5},{5... | collective-permute-start | bytes 786440 | tf_op jit(solution)/shard_map/ppermute | solution.py:13
  443.0 120.7 %all-reduce.20.cloned.1.call-start = ((), (), s32[]{:S(2)}) async-start(), calls=%async_computation.6 | async-start | bytes 524288 | tf_op jit(solution)/shard_map/psum | solution.py:117
  479.7 6.9 %collective-permute-start.17 = (f32[512,128]{1,0:T(8,128)S(1)}, f32[512,128]{1,0:T(8,128)S(1)}, u32[]{:S(2)}, u32[]{:S(2)}) collective-permute-start(f32[512,128]{1,0:T(8,128)S(1)} %constant_dynamic-slice_fusion.1), channel_id=1, source_target_pairs={{0,4},{4,0},{8,12},{12,8},{16,20},{20,16},{24,28},{28,24},{1,5},{5... | collective-permute-start | bytes 786440 | tf_op jit(solution)/shard_map/ppermute | solution.py:13
  486.7 5.0 collective-permute-start.18
  491.7 7.6 %collective-permute-start.19 = (f32[256,128]{1,0:T(8,128)S(1)}, f32[256,128]{1,0:T(8,128)S(1)}, u32[]{:S(2)}, u32[]{:S(2)}) collective-permute-start(f32[256,128]{1,0:T(8,128)S(1)} %dynamic-slice_add_fusion.2), channel_id=1, source_target_pairs={{0,16},{4,20},{8,24},{12,28},{16,0},{20,4},{24,8},{28,12},{1,17},{... | collective-permute-start | bytes 393224 | tf_op jit(solution)/shard_map/ppermute | solution.py:13
  499.4 5.0 collective-permute-start.20
  505.1 6.7 %collective-permute-start.21 = (f32[512,128]{1,0:T(8,128)}, f32[512,128]{1,0:T(8,128)}, u32[]{:S(2)}, u32[]{:S(2)}) collective-permute-start(f32[512,128]{1,0:T(8,128)} %maximum_select_fusion.9), channel_id=1, source_target_pairs={{0,4},{4,0},{8,12},{12,8},{16,20},{20,16},{24,28},{28,24},{1,5},{5... | collective-permute-start | bytes 786440 | tf_op jit(solution)/shard_map/ppermute | solution.py:13
  560.1 2.6 copy-start.5
Sparse Core Ops, SparseCore 0:
  46.0 34.3 all-reduce.7
  119.5 35.1 all-reduce.9
  215.7 51.1 all-reduce.11
  282.1 51.4 all-reduce.13
  371.1 36.4 all-reduce.15
  443.1 33.6 all-reduce.17
  514.9 31.7 all-reduce.19
where the time goes:
time: 575 us; the launch traced here: 573 us
  waiting for transfers between devices  329 us (57%)
  matrix products  82.6 us (14%)
  local copies, waits for them, and re-layouts  56.1 us (10%)
  blocking collectives  39.7 us (7%)
  starting transfers between devices  37.8 us (7%)
  between operations  18.8 us (3%)
  other arithmetic  9.3 us (2%)
    psum x4, waiting for transfers between devices, on_device(): solved_exact = lax.psum(solved_terms, 'rows')  121 us
    psum x3, waiting for transfers between devices, on_device(): right_side = right_side - lax.psum(ancestor_terms, 'rows')  118 us
    ppermute x22, waiting for transfers between devices, swapped(): lax.ppermute(x, axis, [(i, i ^ 1 << apart) for i in range(lax.axis_size(a...  89.8 us
    unnamed x33, local copies, waits for them, and re-layouts  54.7 us
    psum x1, blocking collectives, on_device(): loss_total = lax.psum(loss_sum, ('leaf', 'rows'))  39.7 us
    ppermute x22, starting transfers between devices, swapped(): lax.ppermute(x, axis, [(i, i ^ 1 << apart) for i in range(lax.axis_size(a...  36.9 us
    dot_general x3, matrix products, on_device(): lax.dot_general(couplings[tree_level], solved, contract_rows, preferred_e...  26.5 us
    dot_general x3, matrix products, on_device(): jnp.dot(flat_coupling, stacked, preferred_element_type=jnp.float32)  23.5 us
  transfers between devices with their start and end apart: 29, of which 26 were waited for; matrix products, arithmetic and copies ran while one was open for 10% of the time, Pallas kernels for 0%

commit v1 on v0

v1 whole, which is shorter than its diff:
```python
import functools

import jax
import jax.numpy as jnp
from jax import lax
from jax.experimental import pallas as pl
from jax.experimental.pallas import tpu as pltpu
from jax.sharding import PartitionSpec as P

LEVELS = 4


tail_level = 0.5


def swapped(x, axis, apart):
    return lax.ppermute(x, axis, [(i, i ^ 1 << apart) for i in range(lax.axis_size(axis))])


def bits_of(axis):
    return lax.axis_size(axis).bit_length() - 1


def rows_block(count):
    return min(512, count)


def params():
    return pltpu.CompilerParams(
        dimension_semantics=("arbitrary",), vmem_limit_bytes=24 * 1024 * 1024
    )


def apply_body(has_base, half_ref, *refs):
    if has_base:
        matrix_ref, vector_ref, base_ref, out_ref = refs
    else:
        matrix_ref, vector_ref, out_ref = refs
    product = jnp.dot(matrix_ref[...], vector_ref[...], preferred_element_type=jnp.float32)
    if has_base:
        product = product + base_ref[...]
    out_ref[...] = product


def apply_rows(matrix, plane, vector, base, half, halves):
    _, rows, width = matrix.shape
    count = rows // halves
    block = rows_block(count)
    steps = count // block
    scenarios = vector.shape[1]
    in_specs = [
        pl.BlockSpec((pl.Squeezed(), block, width), lambda i, h: (plane, h[0] * steps + i, 0)),
        pl.BlockSpec((width, scenarios), lambda i, h: (0, 0)),
    ]
    operands = [matrix, vector]
    if base is not None:
        in_specs.append(pl.BlockSpec((block, scenarios), lambda i, h: (h[0] * steps + i, 0)))
        operands.append(base)
    return pl.pallas_call(
        functools.partial(apply_body, base is not None),
        out_shape=jax.ShapeDtypeStruct((count, scenarios), jnp.float32),
        grid_spec=pltpu.PrefetchScalarGridSpec(
            num_scalar_prefetch=1,
            grid=(steps,),
            in_specs=in_specs,
            out_specs=pl.BlockSpec((block, scenarios), lambda i, h: (i, 0)),
        ),
        compiler_params=params(),
    )(half, *operands)


def first_body(half_ref, matrix_ref, noise_ref, out_ref, total_ref):
    step = pl.program_id(0)

    @pl.when(step == 0)
    def _():
        total_ref[...] = jnp.zeros_like(total_ref)

    total_ref[...] += lax.dot_general(
        noise_ref[...], matrix_ref[...], (((0,), (0,)), ((), ())), preferred_element_type=jnp.float32
    )

    @pl.when(step == pl.num_programs(0) - 1)
    def _():
        out_ref[...] = total_ref[...].T


def sample_body(half_steps, half_ref, matrix_ref, noise_ref, own_ref, other_ref, out_ref, total_ref):
    step = pl.program_id(0)

    @pl.when(step == 0)
    def _():
        total_ref[...] = jnp.zeros_like(total_ref)

    def add(terms_ref):
        right = (noise_ref[...].astype(jnp.float32) - terms_ref[...]).astype(jnp.bfloat16)
        total_ref[...] += lax.dot_general(
            right, matrix_ref[...], (((0,), (0,)), ((), ())), preferred_element_type=jnp.float32
        )

    @pl.when(step < half_steps)
    def _():
        add(own_ref)

    @pl.when(step >= half_steps)
    def _():
        add(other_ref)

    @pl.when(step == pl.num_programs(0) - 1)
    def _():
        out_ref[...] = total_ref[...].T


def sample_rows(matrix, noise, own, other, half):
    rows, width = matrix.shape
    scenarios = noise.shape[1]
    if own is None:
        block = rows_block(rows)
        steps = rows // block
        place = lambda i, h: (i, 0)
        body = first_body
        in_specs = [pl.BlockSpec((block, width), place), pl.BlockSpec((block, scenarios), place)]
        operands = [matrix, noise]
    else:
        block = rows_block(rows // 2)
        half_steps = rows // 2 // block
        steps = 2 * half_steps
        place = lambda i, h: ((h[0] * half_steps + i) % steps, 0)
        body = functools.partial(sample_body, half_steps)
        in_specs = [
            pl.BlockSpec((block, width), place),
            pl.BlockSpec((block, scenarios), place),
            pl.BlockSpec((block, scenarios), lambda i, h: (jnp.minimum(i, half_steps - 1), 0)),
            pl.BlockSpec((block, scenarios), lambda i, h: (jnp.maximum(i - half_steps, 0), 0)),
        ]
        operands = [matrix, noise, own, other]
    return pl.pallas_call(
        body,
        out_shape=jax.ShapeDtypeStruct((width, scenarios), jnp.float32),
        grid_spec=pltpu.PrefetchScalarGridSpec(
            num_scalar_prefetch=1,
            grid=(steps,),
            in_specs=in_specs,
            out_specs=pl.BlockSpec((width, scenarios), lambda i, h: (0, 0)),
            scratch_shapes=[pltpu.VMEM((scenarios, width), jnp.float32)],
        ),
        compiler_params=params(),
    )(half, *operands)


def gather_body(half_steps, half_ref, matrix_ref, own_ref, other_ref, out_ref, exact_ref, round_ref, total_ref):
    step = pl.program_id(0)

    @pl.when(step == 0)
    def _():
        total_ref[...] = jnp.zeros_like(total_ref)

    def add(terms_ref):
        exact = terms_ref[...]
        exact_ref[...] = exact
        short = exact.astype(jnp.bfloat16)
        round_ref[...] = short
        total_ref[...] += lax.dot_general(
            short, matrix_ref[...], (((0,), (0,)), ((), ())), preferred_element_type=jnp.float32
        )

    @pl.when(step < half_steps)
    def _():
        add(own_ref)

    @pl.when(step >= half_steps)
    def _():
        add(other_ref)

    @pl.when(step == pl.num_programs(0) - 1)
    def _():
        out_ref[...] = total_ref[...].T


def gather_rows(matrix, plane, own, other, half):
    _, rows, width = matrix.shape
    scenarios = own.shape[1]
    block = rows_block(rows // 2)
    half_steps = rows // 2 // block
    steps = 2 * half_steps
    place = lambda i, h: ((h[0] * half_steps + i) % steps, 0)
    return pl.pallas_call(
        functools.partial(gather_body, half_steps),
        out_shape=(
            jax.ShapeDtypeStruct((width, scenarios), jnp.float32),
            jax.ShapeDtypeStruct((rows, scenarios), jnp.float32),
            jax.ShapeDtypeStruct((rows, scenarios), jnp.bfloat16),
        ),
        grid_spec=pltpu.PrefetchScalarGridSpec(
            num_scalar_prefetch=1,
            grid=(steps,),
            in_specs=[
                pl.BlockSpec(
                    (pl.Squeezed(), block, width), lambda i, h: (plane, (h[0] * half_steps + i) % steps, 0)
                ),
                pl.BlockSpec((block, scenarios), lambda i, h: (jnp.minimum(i, half_steps - 1), 0)),
                pl.BlockSpec((block, scenarios), lambda i, h: (jnp.maximum(i - half_steps, 0), 0)),
            ],
            out_specs=(
                pl.BlockSpec((width, scenarios), lambda i, h: (0, 0)),
                pl.BlockSpec((block, scenarios), place),
                pl.BlockSpec((block, scenarios), place),
            ),
            scratch_shapes=[pltpu.VMEM((scenarios, width), jnp.float32)],
        ),
        compiler_params=params(),
    )(half, matrix, own, other)


def later_body(has_base, matrix_ref, vector_ref, *refs):
    if has_base:
        base_ref, out_ref, total_ref = refs
    else:
        out_ref, total_ref = refs
    step = pl.program_id(0)

    @pl.when(step == 0)
    def _():
        total_ref[...] = jnp.zeros_like(total_ref)

    total_ref[...] += lax.dot_general(
        vector_ref[...], matrix_ref[...], (((0,), (0,)), ((), ())), preferred_element_type=jnp.float32
    )

    @pl.when(step == pl.num_programs(0) - 1)
    def _():
        total = total_ref[...].T
        if has_base:
            total = total + base_ref[...]
        out_ref[...] = total


def later_rows(matrix, plane, vector, base):
    _, rows, width = matrix.shape
    scenarios = vector.shape[1]
    block = rows_block(rows)
    in_specs = [
        pl.BlockSpec((pl.Squeezed(), block, width), lambda i: (plane, i, 0)),
        pl.BlockSpec((block, scenarios), lambda i: (i, 0)),
    ]
    operands = [matrix, vector]
    if base is not None:
        in_specs.append(pl.BlockSpec((width, scenarios), lambda i: (0, 0)))
        operands.append(base)
    return pl.pallas_call(
        functools.partial(later_body, base is not None),
        out_shape=jax.ShapeDtypeStruct((width, scenarios), jnp.float32),
        grid_spec=pltpu.PrefetchScalarGridSpec(
            num_scalar_prefetch=0,
            grid=(rows // block,),
            in_specs=in_specs,
            out_specs=pl.BlockSpec((width, scenarios), lambda i: (0, 0)),
            scratch_shapes=[pltpu.VMEM((scenarios, width), jnp.float32)],
        ),
        compiler_params=params(),
    )(*operands)


def rows_sum(sent, kept):
    own = kept + swapped(sent, "rows", 0)
    for position in range(1, bits_of("rows")):
        own = own + swapped(own, "rows", position)
    return own, swapped(own, "rows", 0)


def halve(value, position, leaf_index):
    half_rows = value.shape[0] // 2
    upper = leaf_index >> position & 1
    kept = lax.dynamic_slice_in_dim(value, upper * half_rows, half_rows, 0)
    sent = lax.dynamic_slice_in_dim(value, (1 - upper) * half_rows, half_rows, 0)
    return kept + swapped(sent, "leaf", position)


def double(value, position, leaf_index):
    partner = swapped(value, "leaf", position)
    upper = leaf_index >> position & 1
    return jnp.where(
        upper == 1,
        jnp.concatenate([partner, value], axis=0),
        jnp.concatenate([value, partner], axis=0),
    )


def group_sum(value, group_bits, leaf_index):
    if group_bits == 0:
        return value
    if group_bits == 1:
        return value + swapped(value, "leaf", 0)
    if group_bits == 2:
        middle = value.shape[0] // 2
        first, second = value[:middle], value[middle:]
        first_got = swapped(first, "leaf", 0)
        second_got = swapped(second, "leaf", 1)
        first, second = first + first_got, second + second_got
        first_got = swapped(first, "leaf", 1)
        second_got = swapped(second, "leaf", 0)
        return jnp.concatenate([first + first_got, second + second_got], axis=0)
    for position in range(2):
        value = halve(value, position, leaf_index)
    for position in range(2, group_bits):
        value = value + swapped(value, "leaf", position)
    for position in reversed(range(2)):
        value = double(value, position, leaf_index)
    return value


def total_sum(value):
    for axis in ("leaf", "rows"):
        for position in range(bits_of(axis)):
            value = value + swapped(value, axis, position)
    return value


def on_device(
    factor_zero,
    factor_one,
    factor_two,
    factor_three,
    coupling_one,
    coupling_two,
    coupling_three,
    noise_zero,
    noise_one,
    noise_two,
    noise_three,
    tail_index,
):
    factors = [factor_zero, factor_one, factor_two, factor_three]
    couplings = [None] + [
        jnp.transpose(coupling, (1, 0, 2)) for coupling in (coupling_one, coupling_two, coupling_three)
    ]
    noises = [noise_zero, noise_one, noise_two, noise_three]
    leaf_bits = bits_of("leaf")
    leaf_index = lax.axis_index("leaf")
    core = (lax.axis_index("rows") & 1).astype(jnp.int32)
    keep_half = core.reshape(1)
    send_half = (1 - core).reshape(1)
    whole = jnp.zeros((1,), jnp.int32)
    full_width = factor_zero.shape[1] * lax.axis_size("rows")
    scenario_count = noise_zero.shape[1]
    columns = jnp.arange(scenario_count, dtype=jnp.int32)
    counts = jnp.sum((tail_index[:, None] == columns[None, :]).astype(jnp.float32), axis=0)
    weights = 1.0 + counts
    samples = []
    early = [None] * LEVELS
    loss_rows = jnp.zeros((8, scenario_count), jnp.float32)
    for tree_level in range(LEVELS):
        group_bits = leaf_bits - tree_level
        own = other = None
        if tree_level > 0:
            coupling = couplings[tree_level]
            last = samples[-1].astype(jnp.bfloat16)
            sent = apply_rows(coupling, tree_level - 1, last, early[tree_level], send_half, 2)
            kept = apply_rows(coupling, tree_level - 1, last, early[tree_level], keep_half, 2)
            own, other = rows_sum(sent, kept)
            for deeper in range(tree_level + 1, LEVELS):
                early[deeper] = apply_rows(
                    couplings[deeper], tree_level - 1, last, early[deeper], whole, 1
                )
        partial_sample = sample_rows(factors[tree_level], noises[tree_level], own, other, keep_half)
        sample = group_sum(partial_sample, group_bits, leaf_index)
        samples.append(sample)
        piece_rows = sample.shape[0] >> group_bits
        member = leaf_index & (1 << group_bits) - 1
        own_rows = lax.dynamic_slice_in_dim(sample, member * piece_rows, piece_rows, 0)
        losses = weights[None, :] * jax.nn.softplus(own_rows - tail_level)
        loss_rows = loss_rows + jnp.sum(losses.reshape(-1, 8, scenario_count), axis=0)
    loss_total = jnp.sum(total_sum(loss_rows))
    tail_loss = loss_total / jnp.float32(
        (2**LEVELS - 1) * full_width * (scenario_count + tail_index.shape[0])
    )
    pending = [None] * LEVELS
    gradients = [None] * LEVELS
    for tree_level in reversed(range(LEVELS)):
        group_bits = leaf_bits - tree_level
        adjoint = weights[None, :] * jax.nn.sigmoid(samples[tree_level] - tail_level)
        if tree_level < LEVELS - 1:
            adjoint = adjoint - group_sum(pending[tree_level], group_bits, leaf_index)
        adjoint_round = adjoint.astype(jnp.bfloat16)
        factor = factors[tree_level][None]
        sent = apply_rows(factor, 0, adjoint_round, None, send_half, 2)
        kept = apply_rows(factor, 0, adjoint_round, None, keep_half, 2)
        own, other = rows_sum(sent, kept)
        if tree_level > 0:
            upward, gradients[tree_level], solved = gather_rows(
                couplings[tree_level], tree_level - 1, own, other, keep_half
            )
            before = pending[tree_level - 1]
            pending[tree_level - 1] = upward if before is None else before + upward
            for ancestor in range(tree_level - 1):
                pending[ancestor] = later_rows(
                    couplings[tree_level], ancestor, solved, pending[ancestor]
                )
        else:
            gradients[0] = jnp.where(
                core == 1,
                jnp.concatenate([other, own], axis=0),
                jnp.concatenate([own, other], axis=0),
            )
    return (gradients[0], gradients[1], gradients[2], gradients[3], tail_loss)


def solution(mesh):
    in_specs = (
        P("leaf", "rows"),
        P("leaf", "rows"),
        P("leaf", "rows"),
        P("leaf", "rows"),
        P("leaf", None, "rows"),
        P("leaf", None, "rows"),
        P("leaf", None, "rows"),
        P("leaf", None),
        P("leaf", None),
        P("leaf", None),
        P("leaf", None),
        P(),
    )
    out_specs = (P("leaf", None), P("leaf", None), P("leaf", None), P("leaf", None), P())
    return jax.shard_map(
        on_device, mesh=mesh, in_specs=in_specs, out_specs=out_specs, check_vma=False
    )
```

time: 575 us -> 372 us (0.65)
  waiting for transfers between devices: 329 us -> 195 us
  matrix products: 82.6 us -> 0 us
  Pallas kernels: 0 us -> 45 us
  blocking collectives: 39.7 us -> 0 us
  local copies, waits for them, and re-layouts: 56.1 us -> 73.5 us
  between operations: 18.8 us -> 3.21 us
  starting transfers between devices: 37.8 us -> 44.5 us
    psum x7 -> x0, waiting for transfers between devices: 239 us -> none  [the longest x4 121 us: on_device(): solved_exact = lax.psum(solved_terms, 'rows')]
    ppermute x22 -> x46, waiting for transfers between devices: 89.8 us -> 195 us  [swapped(): lax.ppermute(x, axis, [(i, i ^ 1 << apart) for i in range(lax.axis_size(a...]
    dot_general x14 -> x0, matrix products: 82.6 us -> none  [the longest x3 26.5 us: on_device(): lax.dot_general(couplings[tree_level], solved, contract_rows, preferred_e...]
    pallas_call x0 -> x27, Pallas kernels: none -> 45 us  [the longest x17 21.8 us: apply_rows(): pl.pallas_call(functools.partial(apply_body, base is not None), out_shape...]
    psum x1 -> x0, blocking collectives: 39.7 us -> none  [on_device(): loss_total = lax.psum(loss_sum, ('leaf', 'rows'))]
    unnamed x33 -> x63, local copies, waits for them, and re-layouts: 54.7 us -> 73.3 us
    ppermute x22 -> x46, starting transfers between devices: 36.9 us -> 44.5 us  [swapped(): lax.ppermute(x, axis, [(i, i ^ 1 << apart) for i in range(lax.axis_size(a...]
  transfers between devices with their start and end apart: 29 -> 46, of which waited for: 26 -> 38; matrix products, arithmetic and copies ran while one was open for 10% -> 3% of each run, Pallas kernels for 0% -> 6%
where the time goes in v1:
time: 372 us; the launch traced here: 371 us
  waiting for transfers between devices  195 us (52%)
  local copies, waits for them, and re-layouts  73.5 us (20%)
  Pallas kernels  45 us (12%)
  starting transfers between devices  44.5 us (12%)
  other arithmetic  10.1 us (3%)
    ppermute x46, waiting for transfers between devices, swapped(): lax.ppermute(x, axis, [(i, i ^ 1 << apart) for i in range(lax.axis_size(a...  195 us
    unnamed x63, local copies, waits for them, and re-layouts  73.3 us
    ppermute x46, starting transfers between devices, swapped(): lax.ppermute(x, axis, [(i, i ^ 1 << apart) for i in range(lax.axis_size(a...  44.5 us
    pallas_call x17, Pallas kernels, apply_rows(): pl.pallas_call(functools.partial(apply_body, base is not None), out_shape...  21.8 us
    pallas_call x3, Pallas kernels, gather_rows(): pl.pallas_call(functools.partial(gather_body, half_steps), out_shape=(jax...  9.35 us
    pallas_call x3, Pallas kernels, later_rows(): pl.pallas_call(functools.partial(later_body, base is not None), out_shape...  7.68 us
  transfers between devices with their start and end apart: 46, of which 38 were waited for; matrix products, arithmetic and copies ran while one was open for 3% of the time, Pallas kernels for 6%

profile of v1, /device:TPU:0, one launch (start us, length us, event | category | flops | bytes accessed | tf_op | source)
XLA Modules:
  0.0 371.3 jit_solution(12135238385944489887)
XLA Ops:
  3.2 3.0 collective-permute-start
  6.3 6.3 %collective-permute-done = f32[512,128]{1,0:T(8,128)S(1)} collective-permute-done((f32[512,128]{1,0:T(8,128)S(1)}, f32[512,128]{1,0:T(8,128)S(1)}, u32[]{:S(2)}, u32[]{:S(2)}) %collective-permute-start) | collective-permute-done | bytes 262176 | tf_op jit(solution)/shard_map/ppermute | solution.py:17
  12.6 1.9 collective-permute-start.1
  14.5 3.2 collective-permute-done.1
  17.7 2.9 collective-permute-start.2
  20.6 4.6 %collective-permute-done.2 = f32[256,128]{1,0:T(8,128)S(1)} collective-permute-done((f32[256,128]{1,0:T(8,128)S(1)}, f32[256,128]{1,0:T(8,128)S(1)}, u32[]{:S(2)}, u32[]{:S(2)}) %collective-permute-start.2) | collective-permute-done | bytes 131104 | tf_op jit(solution)/shard_map/ppermute | solution.py:17
  26.0 4.2 %collective-permute-done.3 = f32[256,128]{1,0:T(8,128)S(1)} collective-permute-done((f32[256,128]{1,0:T(8,128)S(1)}, f32[256,128]{1,0:T(8,128)S(1)}, u32[]{:S(2)}, u32[]{:S(2)}) %collective-permute-start.3) | collective-permute-done | bytes 131104 | tf_op jit(solution)/shard_map/ppermute | solution.py:17
  30.2 1.8 collective-permute-start.4
  32.0 4.6 %collective-permute-done.4 = f32[512,128]{1,0:T(8,128)S(1)} collective-permute-done((f32[512,128]{1,0:T(8,128)S(1)}, f32[512,128]{1,0:T(8,128)S(1)}, u32[]{:S(2)}, u32[]{:S(2)}) %collective-permute-start.4) | collective-permute-done | bytes 262176 | tf_op jit(solution)/shard_map/ppermute | solution.py:17
  43.5 7.0 %collective-permute-done.6 = f32[512,128]{1,0:T(8,128)S(1)} collective-permute-done((f32[512,128]{1,0:T(8,128)S(1)}, f32[512,128]{1,0:T(8,128)S(1)}, u32[]{:S(2)}, u32[]{:S(2)}) %collective-permute-start.6) | collective-permute-done | bytes 262176 | tf_op jit(solution)/shard_map/ppermute | solution.py:17
  55.5 6.0 %collective-permute-done.10 = f32[512,128]{1,0:T(8,128)S(1)} collective-permute-done((f32[512,128]{1,0:T(8,128)S(1)}, f32[512,128]{1,0:T(8,128)S(1)}, u32[]{:S(2)}, u32[]{:S(2)}) %collective-permute-start.10) | collective-permute-done | bytes 262176 | tf_op jit(solution)/shard_map/ppermute | solution.py:17
  65.2 9.4 %copy.20 = bf16[2048,2,1024]{2,0,1:T(8,128)(2,1)} copy(bf16[2048,2,1024]{2,1,0:T(2,128)(2,1)} %param.17) | data formatting | bytes 16777216 | tf_op args[5]
  74.5 3.4 copy-done.5
  85.9 12.5 %collective-permute-done.13 = f32[1024,128]{1,0:T(8,128)S(1)} collective-permute-done((f32[1024,128]{1,0:T(8,128)S(1)}, f32[1024,128]{1,0:T(8,128)S(1)}, u32[]{:S(2)}, u32[]{:S(2)}) %collective-permute-start.13) | collective-permute-done | bytes 524320 | tf_op jit(solution)/shard_map/ppermute | solution.py:17
  98.5 1.9 collective-permute-done.14.other_ref
  102.5 8.2 %copy-done = bf16[4096,3,1024]{2,0,1:T(8,128)(2,1)S(1)} copy-done((bf16[4096,3,1024]{2,0,1:T(8,128)(2,1)S(1)}, bf16[4096,3,1024]{2,0,1:T(8,128)(2,1)}, u32[]{:S(2)}) %copy-start) | copy-done | bytes 25165848
  110.6 3.5 shard_map.163.refs_2_
  114.1 3.5 shard_map.164.refs_2_
  119.0 1.9 fusion.18
  120.9 8.2 %copy-done.1 = bf16[4096,3,1024]{2,0,1:T(8,128)(2,1)S(1)} copy-done((bf16[4096,3,1024]{2,0,1:T(8,128)(2,1)S(1)}, bf16[4096,3,1024]{2,0,1:T(8,128)(2,1)}, u32[]{:S(2)}) %copy-start.1) | copy-done | bytes 25165848
  138.4 23.5 %collective-permute-done.17 = f32[2048,128]{1,0:T(8,128)S(1)} collective-permute-done((f32[2048,128]{1,0:T(8,128)S(1)}, f32[2048,128]{1,0:T(8,128)S(1)}, u32[]{:S(2)}, u32[]{:S(2)}) %collective-permute-start.17) | collective-permute-done | bytes 1048608 | tf_op jit(solution)/shard_map/ppermute | solution.py:17
  162.2 2.5 collective-permute-done.18.other_ref
  164.7 3.4 copy-done.7
  168.1 3.1 shard_map.167
  177.8 23.5 %collective-permute-done.20 = f32[2048,128]{1,0:T(8,128)S(1)} collective-permute-done((f32[2048,128]{1,0:T(8,128)S(1)}, f32[2048,128]{1,0:T(8,128)S(1)}, u32[]{:S(2)}, u32[]{:S(2)}) %collective-permute-start.20) | collective-permute-done | bytes 1048608 | tf_op jit(solution)/shard_map/ppermute | solution.py:17
  205.1 8.2 %copy-done.2 = bf16[4096,3,1024]{2,0,1:T(8,128)(2,1)S(1)} copy-done((bf16[4096,3,1024]{2,0,1:T(8,128)(2,1)S(1)}, bf16[4096,3,1024]{2,0,1:T(8,128)(2,1)}, u32[]{:S(2)}) %copy-start.2) | copy-done | bytes 25165848
  215.7 4.8 %shard_map.170 = (f32[1024,128]{1,0:T(8,128)S(1)}, f32[4096,128]{1,0:T(8,128)}, bf16[4096,128]{1,0:T(8,128)(2,1)S(1)}) custom-call(s32[1]{0:T(128)} %bitcast.half_ref, bf16[3,4096,1024]{2,1,0:T(8,128)(2,1)S(1)} %bitcast.31, f32[2048,128]{1,0:T(8,128)S(1)} %copy-done.19, f32[2048,128]{1,0:T(8,128)S(1)} %copy-done.22), custom_call_target="tpu_custom_call" | custom-call | tf_op jit(solution)/shard_map/pallas_call | solution.py:187
  222.3 12.2 %collective-permute-done.22 = f32[1024,128]{1,0:T(8,128)S(1)} collective-permute-done((f32[1024,128]{1,0:T(8,128)S(1)}, f32[1024,128]{1,0:T(8,128)S(1)}, u32[]{:S(2)}, u32[]{:S(2)}) %collective-permute-start.22) | collective-permute-done | bytes 524320 | tf_op jit(solution)/shard_map/ppermute | solution.py:17
  234.7 2.2 copy-done.9
  241.6 12.3 %collective-permute-done.24 = f32[1024,128]{1,0:T(8,128)S(1)} collective-permute-done((f32[1024,128]{1,0:T(8,128)S(1)}, f32[1024,128]{1,0:T(8,128)S(1)}, u32[]{:S(2)}, u32[]{:S(2)}) %collective-permute-start.24) | collective-permute-done | bytes 524320 | tf_op jit(solution)/shard_map/ppermute | solution.py:17
  254.0 8.1 %copy-done.3 = bf16[4096,3,1024]{2,0,1:T(8,128)(2,1)S(1)} copy-done((bf16[4096,3,1024]{2,0,1:T(8,128)(2,1)S(1)}, bf16[4096,3,1024]{2,0,1:T(8,128)(2,1)}, u32[]{:S(2)}) %copy-start.3) | copy-done | bytes 25165848
  262.2 3.0 shard_map.176
  265.2 2.8 shard_map.173
  270.4 6.4 %collective-permute-done.26 = f32[512,128]{1,0:T(8,128)S(1)} collective-permute-done((f32[512,128]{1,0:T(8,128)S(1)}, f32[512,128]{1,0:T(8,128)S(1)}, u32[]{:S(2)}, u32[]{:S(2)}) %collective-permute-start.26) | collective-permute-done | bytes 262176 | tf_op jit(solution)/shard_map/ppermute | solution.py:17
  279.5 6.5 %collective-permute-done.27 = f32[512,128]{1,0:T(8,128)S(1)} collective-permute-done((f32[512,128]{1,0:T(8,128)S(1)}, f32[512,128]{1,0:T(8,128)S(1)}, u32[]{:S(2)}, u32[]{:S(2)}) %collective-permute-start.27) | collective-permute-done | bytes 262176 | tf_op jit(solution)/shard_map/ppermute | solution.py:17
  290.2 6.9 %collective-permute-done.31 = f32[512,128]{1,0:T(8,128)S(1)} collective-permute-done((f32[512,128]{1,0:T(8,128)S(1)}, f32[512,128]{1,0:T(8,128)S(1)}, u32[]{:S(2)}, u32[]{:S(2)}) %collective-permute-start.31) | collective-permute-done | bytes 262176 | tf_op jit(solution)/shard_map/ppermute | solution.py:17
  297.2 8.1 %copy-done.4 = bf16[4096,3,1024]{2,0,1:T(8,128)(2,1)S(1)} copy-done((bf16[4096,3,1024]{2,0,1:T(8,128)(2,1)S(1)}, bf16[4096,3,1024]{2,0,1:T(8,128)(2,1)}, u32[]{:S(2)}) %copy-start.4) | copy-done | bytes 25165848
  305.3 3.0 shard_map.174.refs_0_
  312.6 8.1 %collective-permute-done.33 = f32[512,128]{1,0:T(8,128)S(1)} collective-permute-done((f32[512,128]{1,0:T(8,128)S(1)}, f32[512,128]{1,0:T(8,128)S(1)}, u32[]{:S(2)}, u32[]{:S(2)}) %collective-permute-start.33) | collective-permute-done | bytes 262176 | tf_op jit(solution)/shard_map/ppermute | solution.py:17
  322.3 3.7 collective-permute-done.34
  326.0 3.5 collective-permute-start.35
  329.5 5.3 %collective-permute-done.35 = f32[256,128]{1,0:T(8,128)S(1)} collective-permute-done((f32[256,128]{1,0:T(8,128)S(1)}, f32[256,128]{1,0:T(8,128)S(1)}, u32[]{:S(2)}, u32[]{:S(2)}) %collective-permute-start.35) | collective-permute-done | bytes 131104 | tf_op jit(solution)/shard_map/ppermute | solution.py:17
  334.9 5.0 %collective-permute-done.36 = f32[256,128]{1,0:T(8,128)S(1)} collective-permute-done((f32[256,128]{1,0:T(8,128)S(1)}, f32[256,128]{1,0:T(8,128)S(1)}, u32[]{:S(2)}, u32[]{:S(2)}) %collective-permute-start.36) | collective-permute-done | bytes 131104 | tf_op jit(solution)/shard_map/ppermute | solution.py:17
  341.8 4.8 %collective-permute-done.37 = f32[512,128]{1,0:T(8,128)S(1)} collective-permute-done((f32[512,128]{1,0:T(8,128)S(1)}, f32[512,128]{1,0:T(8,128)S(1)}, u32[]{:S(2)}, u32[]{:S(2)}) %collective-permute-start.37) | collective-permute-done | bytes 262176 | tf_op jit(solution)/shard_map/ppermute | solution.py:17
  351.7 3.5 collective-permute-done.39
  356.2 2.7 collective-permute-done.42
  359.6 3.8 %collective-permute-done.43 = f32[8,128]{1,0:T(8,128)S(1)} collective-permute-done((f32[8,128]{1,0:T(8,128)S(1)}, f32[8,128]{1,0:T(8,128)S(1)}, u32[]{:S(2)}, u32[]{:S(2)}) %collective-permute-start.43) | collective-permute-done | bytes 4128 | tf_op jit(solution)/shard_map/ppermute | solution.py:17
  366.1 2.1 collective-permute-done.45
  (190 shorter events, 87.3 us)
Async XLA Ops:
  3.2 9.3 %collective-permute-start = (f32[512,128]{1,0:T(8,128)S(1)}, f32[512,128]{1,0:T(8,128)S(1)}, u32[]{:S(2)}, u32[]{:S(2)}) collective-permute-start(f32[512,128]{1,0:T(8,128)S(1)} %constant_dynamic-slice_fusion.3), channel_id=1, source_target_pairs={{0,4},{4,0},{8,12},{12,8},{16,20},{20,16},{24,28},{28,24},{1,5},{5... | collective-permute-start | bytes 786440 | tf_op jit(solution)/shard_map/ppermute | solution.py:17
  12.6 5.0 %collective-permute-start.1 = (f32[256,128]{1,0:T(8,128)S(1)}, f32[256,128]{1,0:T(8,128)S(1)}, u32[]{:S(2)}, u32[]{:S(2)}) collective-permute-start(f32[256,128]{1,0:T(8,128)S(1)} %constant_dynamic-slice_fusion.2), channel_id=1, source_target_pairs={{0,8},{4,12},{8,0},{12,4},{16,24},{20,28},{24,16},{28,20},{1,9},{5... | collective-permute-start | bytes 393224 | tf_op jit(solution)/shard_map/ppermute | solution.py:17
  17.7 7.4 %collective-permute-start.2 = (f32[256,128]{1,0:T(8,128)S(1)}, f32[256,128]{1,0:T(8,128)S(1)}, u32[]{:S(2)}, u32[]{:S(2)}) collective-permute-start(f32[256,128]{1,0:T(8,128)S(1)} %dynamic-slice_add_fusion.3), channel_id=1, source_target_pairs={{0,16},{4,20},{8,24},{12,28},{16,0},{20,4},{24,8},{28,12},{1,17},{... | collective-permute-start | bytes 393224 | tf_op jit(solution)/shard_map/ppermute | solution.py:17
  25.2 5.0 %collective-permute-start.3 = (f32[256,128]{1,0:T(8,128)S(1)}, f32[256,128]{1,0:T(8,128)S(1)}, u32[]{:S(2)}, u32[]{:S(2)}) collective-permute-start(f32[256,128]{1,0:T(8,128)S(1)} %add.198), channel_id=1, source_target_pairs={{0,8},{4,12},{8,0},{12,4},{16,24},{20,28},{24,16},{28,20},{1,9},{5... | collective-permute-start | bytes 393224 | tf_op jit(solution)/shard_map/ppermute | solution.py:17
  30.2 6.4 %collective-permute-start.4 = (f32[512,128]{1,0:T(8,128)S(1)}, f32[512,128]{1,0:T(8,128)S(1)}, u32[]{:S(2)}, u32[]{:S(2)}) collective-permute-start(f32[512,128]{1,0:T(8,128)S(1)} %maximum_select_fusion.2), channel_id=1, source_target_pairs={{0,4},{4,0},{8,12},{12,8},{16,20},{20,16},{24,28},{28,24},{1,5},{5... | collective-permute-start | bytes 786440 | tf_op jit(solution)/shard_map/ppermute | solution.py:17
  39.6 2.1 collective-permute-start.5
  41.7 8.8 %collective-permute-start.6 = (f32[512,128]{1,0:T(8,128)S(1)}, f32[512,128]{1,0:T(8,128)S(1)}, u32[]{:S(2)}, u32[]{:S(2)}) collective-permute-start(f32[512,128]{1,0:T(8,128)S(1)} %add.200), channel_id=1, source_target_pairs={{0,2},{1,3},{2,0},{3,1},{4,6},{5,7},{6,4},{7,5},{8,10},{9,11},{10,... | collective-permute-start | bytes 786440 | tf_op jit(solution)/shard_map/ppermute | solution.py:17
  50.5 1.6 collective-permute-start.7
  53.2 8.4 %collective-permute-start.10 = (f32[512,128]{1,0:T(8,128)S(1)}, f32[512,128]{1,0:T(8,128)S(1)}, u32[]{:S(2)}, u32[]{:S(2)}) collective-permute-start(f32[512,128]{1,0:T(8,128)S(1)} %get-tuple-element.32), channel_id=1, source_target_pairs={{0,8},{4,12},{8,0},{12,4},{16,24},{20,28},{24,16},{28,20},{1,9},{5... | collective-permute-start | bytes 786440 | tf_op jit(solution)/shard_map/ppermute | solution.py:17
  54.0 8.1 %collective-permute-start.8 = (f32[512,128]{1,0:T(8,128)S(1)}, f32[512,128]{1,0:T(8,128)S(1)}, u32[]{:S(2)}, u32[]{:S(2)}) collective-permute-start(f32[512,128]{1,0:T(8,128)S(1)} %get-tuple-element.31), channel_id=1, source_target_pairs={{0,4},{4,0},{8,12},{12,8},{16,20},{20,16},{24,28},{28,24},{1,5},{5... | collective-permute-start | bytes 786440 | tf_op jit(solution)/shard_map/ppermute | solution.py:17
  62.1 17.5 %collective-permute-start.9 = (f32[512,128]{1,0:T(8,128)S(1)}, f32[512,128]{1,0:T(8,128)S(1)}, u32[]{:S(2)}, u32[]{:S(2)}) collective-permute-start(f32[512,128]{1,0:T(8,128)S(1)} %get-tuple-element.29), channel_id=1, source_target_pairs={{0,8},{4,12},{8,0},{12,4},{16,24},{20,28},{24,16},{28,20},{1,9},{5... | collective-permute-start | bytes 786440 | tf_op jit(solution)/shard_map/ppermute | solution.py:17
  63.4 16.3 %collective-permute-start.11 = (f32[512,128]{1,0:T(8,128)S(1)}, f32[512,128]{1,0:T(8,128)S(1)}, u32[]{:S(2)}, u32[]{:S(2)}) collective-permute-start(f32[512,128]{1,0:T(8,128)S(1)} %get-tuple-element.30), channel_id=1, source_target_pairs={{0,4},{4,0},{8,12},{12,8},{16,20},{20,16},{24,28},{28,24},{1,5},{5... | collective-permute-start | bytes 786440 | tf_op jit(solution)/shard_map/ppermute | solution.py:17
  82.3 2.0 collective-permute-start.12
  84.3 14.0 %collective-permute-start.13 = (f32[1024,128]{1,0:T(8,128)S(1)}, f32[1024,128]{1,0:T(8,128)S(1)}, u32[]{:S(2)}, u32[]{:S(2)}) collective-permute-start(f32[1024,128]{1,0:T(8,128)S(1)} %add.206), channel_id=1, source_target_pairs={{0,2},{1,3},{2,0},{3,1},{4,6},{5,7},{6,4},{7,5},{8,10},{9,11},{10,... | collective-permute-start | bytes 1572872 | tf_op jit(solution)/shard_map/ppermute | solution.py:17
  98.4 2.0 collective-permute-start.14
  102.1 16.9 %collective-permute-start.15 = (f32[1024,128]{1,0:T(8,128)S(1)}, f32[1024,128]{1,0:T(8,128)}, u32[]{:S(2)}, u32[]{:S(2)}) collective-permute-start(f32[1024,128]{1,0:T(8,128)S(1)} %shard_map.162), channel_id=1, source_target_pairs={{0,4},{4,0},{8,12},{12,8},{16,20},{20,16},{24,28},{28,24},{1,5},{5... | collective-permute-start | bytes 1572872 | tf_op jit(solution)/shard_map/ppermute | solution.py:17
  132.4 2.9 collective-permute-start.16
  136.6 25.3 %collective-permute-start.17 = (f32[2048,128]{1,0:T(8,128)S(1)}, f32[2048,128]{1,0:T(8,128)S(1)}, u32[]{:S(2)}, u32[]{:S(2)}) collective-permute-start(f32[2048,128]{1,0:T(8,128)S(1)} %add.210), channel_id=1, source_target_pairs={{0,2},{1,3},{2,0},{3,1},{4,6},{5,7},{6,4},{7,5},{8,10},{9,11},{10,... | collective-permute-start | bytes 3145736 | tf_op jit(solution)/shard_map/ppermute | solution.py:17
  162.0 2.7 collective-permute-start.18
  173.2 2.7 collective-permute-start.19
  176.0 25.3 %collective-permute-start.20 = (f32[2048,128]{1,0:T(8,128)S(1)}, f32[2048,128]{1,0:T(8,128)S(1)}, u32[]{:S(2)}, u32[]{:S(2)}) collective-permute-start(f32[2048,128]{1,0:T(8,128)S(1)} %add.213), channel_id=1, source_target_pairs={{0,2},{1,3},{2,0},{3,1},{4,6},{5,7},{6,4},{7,5},{8,10},{9,11},{10,... | collective-permute-start | bytes 3145736 | tf_op jit(solution)/shard_map/ppermute | solution.py:17
  201.3 33.2 %copy-start.28 = (f32[1024,128]{1,0:T(8,128)S(1)}, f32[1024,128]{1,0:T(8,128)}, u32[]{:S(2)}) copy-start(f32[1024,128]{1,0:T(8,128)} %get-tuple-element.22) | copy-start | bytes 1572868
  201.4 2.7 collective-permute-start.21
  220.5 14.0 %collective-permute-start.22 = (f32[1024,128]{1,0:T(8,128)S(1)}, f32[1024,128]{1,0:T(8,128)S(1)}, u32[]{:S(2)}, u32[]{:S(2)}) collective-permute-start(f32[1024,128]{1,0:T(8,128)S(1)} %get-tuple-element.13), channel_id=1, source_target_pairs={{0,4},{4,0},{8,12},{12,8},{16,20},{20,16},{24,28},{28,24},{1,5},{5... | collective-permute-start | bytes 1572872 | tf_op jit(solution)/shard_map/ppermute | solution.py:17
  237.8 2.0 collective-permute-start.23
  239.8 14.0 %collective-permute-start.24 = (f32[1024,128]{1,0:T(8,128)S(1)}, f32[1024,128]{1,0:T(8,128)S(1)}, u32[]{:S(2)}, u32[]{:S(2)}) collective-permute-start(f32[1024,128]{1,0:T(8,128)S(1)} %add.216), channel_id=1, source_target_pairs={{0,2},{1,3},{2,0},{3,1},{4,6},{5,7},{6,4},{7,5},{8,10},{9,11},{10,... | collective-permute-start | bytes 1572872 | tf_op jit(solution)/shard_map/ppermute | solution.py:17
  253.9 11.3 %collective-permute-start.25 = (f32[1024,128]{1,0:T(8,128)S(1)}, f32[1024,128]{1,0:T(8,128)S(1)}, u32[]{:S(2)}, u32[]{:S(2)}) collective-permute-start(f32[1024,128]{1,0:T(8,128)S(1)} %add.217.own_ref), channel_id=1, source_target_pairs={{0,1},{1,0},{2,3},{3,2},{4,5},{5,4},{6,7},{7,6},{8,9},{9,8},{10,11... | collective-permute-start | bytes 1572872 | tf_op jit(solution)/shard_map/ppermute | solution.py:17
  268.1 8.8 %collective-permute-start.26 = (f32[512,128]{1,0:T(8,128)S(1)}, f32[512,128]{1,0:T(8,128)S(1)}, u32[]{:S(2)}, u32[]{:S(2)}) collective-permute-start(f32[512,128]{1,0:T(8,128)S(1)} %get-tuple-element.27), channel_id=1, source_target_pairs={{0,4},{4,0},{8,12},{12,8},{16,20},{20,16},{24,28},{28,24},{1,5},{5... | collective-permute-start | bytes 786440 | tf_op jit(solution)/shard_map/ppermute | solution.py:17
  269.9 8.4 %collective-permute-start.28 = (f32[512,128]{1,0:T(8,128)S(1)}, f32[512,128]{1,0:T(8,128)S(1)}, u32[]{:S(2)}, u32[]{:S(2)}) collective-permute-start(f32[512,128]{1,0:T(8,128)S(1)} %get-tuple-element.28), channel_id=1, source_target_pairs={{0,8},{4,12},{8,0},{12,4},{16,24},{20,28},{24,16},{28,20},{1,9},{5... | collective-permute-start | bytes 786440 | tf_op jit(solution)/shard_map/ppermute | solution.py:17
  278.4 7.7 %collective-permute-start.27 = (f32[512,128]{1,0:T(8,128)S(1)}, f32[512,128]{1,0:T(8,128)S(1)}, u32[]{:S(2)}, u32[]{:S(2)}) collective-permute-start(f32[512,128]{1,0:T(8,128)S(1)} %get-tuple-element.25), channel_id=1, source_target_pairs={{0,8},{4,12},{8,0},{12,4},{16,24},{20,28},{24,16},{28,20},{1,9},{5... | collective-permute-start | bytes 786440 | tf_op jit(solution)/shard_map/ppermute | solution.py:17
  279.0 7.3 %collective-permute-start.29 = (f32[512,128]{1,0:T(8,128)S(1)}, f32[512,128]{1,0:T(8,128)S(1)}, u32[]{:S(2)}, u32[]{:S(2)}) collective-permute-start(f32[512,128]{1,0:T(8,128)S(1)} %get-tuple-element.26), channel_id=1, source_target_pairs={{0,4},{4,0},{8,12},{12,8},{16,20},{20,16},{24,28},{28,24},{1,5},{5... | collective-permute-start | bytes 786440 | tf_op jit(solution)/shard_map/ppermute | solution.py:17
  287.0 1.6 collective-permute-start.30
  288.6 8.4 %collective-permute-start.31 = (f32[512,128]{1,0:T(8,128)S(1)}, f32[512,128]{1,0:T(8,128)S(1)}, u32[]{:S(2)}, u32[]{:S(2)}) collective-permute-start(f32[512,128]{1,0:T(8,128)S(1)} %add.224), channel_id=1, source_target_pairs={{0,2},{1,3},{2,0},{3,1},{4,6},{5,7},{6,4},{7,5},{8,10},{9,11},{10,... | collective-permute-start | bytes 786440 | tf_op jit(solution)/shard_map/ppermute | solution.py:17
  297.1 13.0 %collective-permute-start.32 = (f32[512,128]{1,0:T(8,128)S(1)}, f32[512,128]{1,0:T(8,128)S(1)}, u32[]{:S(2)}, u32[]{:S(2)}) collective-permute-start(f32[512,128]{1,0:T(8,128)S(1)} %add.225.own_ref), channel_id=1, source_target_pairs={{0,1},{1,0},{2,3},{3,2},{4,5},{5,4},{6,7},{7,6},{8,9},{9,8},{10,11... | collective-permute-start | bytes 786440 | tf_op jit(solution)/shard_map/ppermute | solution.py:17
  310.0 37.8 %copy-start.17 = (bf16[512,1024]{1,0:T(8,128)(2,1)S(1)}, bf16[512,1024]{1,0:T(8,128)(2,1)}, u32[]{:S(2)}) copy-start(bf16[512,1024]{1,0:T(8,128)(2,1)} %matrix_ref.4) | copy-start | bytes 3145732
  311.9 8.8 %collective-permute-start.33 = (f32[512,128]{1,0:T(8,128)S(1)}, f32[512,128]{1,0:T(8,128)S(1)}, u32[]{:S(2)}, u32[]{:S(2)}) collective-permute-start(f32[512,128]{1,0:T(8,128)S(1)} %constant_dynamic-slice_fusion.1), channel_id=1, source_target_pairs={{0,4},{4,0},{8,12},{12,8},{16,20},{20,16},{24,28},{28,24},{1,5},{5... | collective-permute-start | bytes 786440 | tf_op jit(solution)/shard_map/ppermute | solution.py:17
  320.8 5.2 %collective-permute-start.34 = (f32[256,128]{1,0:T(8,128)S(1)}, f32[256,128]{1,0:T(8,128)S(1)}, u32[]{:S(2)}, u32[]{:S(2)}) collective-permute-start(f32[256,128]{1,0:T(8,128)S(1)} %constant_dynamic-slice_fusion), channel_id=1, source_target_pairs={{0,8},{4,12},{8,0},{12,4},{16,24},{20,28},{24,16},{28,20},{1,9},{5... | collective-permute-start | bytes 393224 | tf_op jit(solution)/shard_map/ppermute | solution.py:17
  326.0 8.8 %collective-permute-start.35 = (f32[256,128]{1,0:T(8,128)S(1)}, f32[256,128]{1,0:T(8,128)S(1)}, u32[]{:S(2)}, u32[]{:S(2)}) collective-permute-start(f32[256,128]{1,0:T(8,128)S(1)} %dynamic-slice_add_fusion.2), channel_id=1, source_target_pairs={{0,16},{4,20},{8,24},{12,28},{16,0},{20,4},{24,8},{28,12},{1,17},{... | collective-permute-start | bytes 393224 | tf_op jit(solution)/shard_map/ppermute | solution.py:17
  334.8 5.1 %collective-permute-start.36 = (f32[256,128]{1,0:T(8,128)S(1)}, f32[256,128]{1,0:T(8,128)S(1)}, u32[]{:S(2)}, u32[]{:S(2)}) collective-permute-start(f32[256,128]{1,0:T(8,128)S(1)} %add.229), channel_id=1, source_target_pairs={{0,8},{4,12},{8,0},{12,4},{16,24},{20,28},{24,16},{28,20},{1,9},{5... | collective-permute-start | bytes 393224 | tf_op jit(solution)/shard_map/ppermute | solution.py:17
  339.9 6.7 %collective-permute-start.37 = (f32[512,128]{1,0:T(8,128)S(1)}, f32[512,128]{1,0:T(8,128)S(1)}, u32[]{:S(2)}, u32[]{:S(2)}) collective-permute-start(f32[512,128]{1,0:T(8,128)S(1)} %maximum_select_fusion.3), channel_id=1, source_target_pairs={{0,4},{4,0},{8,12},{12,8},{16,20},{20,16},{24,28},{28,24},{1,5},{5... | collective-permute-start | bytes 786440 | tf_op jit(solution)/shard_map/ppermute | solution.py:17
  348.1 1.4 collective-permute-start.38
  349.5 5.6 %collective-permute-start.39 = (f32[256,128]{1,0:T(8,128)S(1)}, f32[256,128]{1,0:T(8,128)S(1)}, u32[]{:S(2)}, u32[]{:S(2)}) collective-permute-start(f32[256,128]{1,0:T(8,128)S(1)} %add.230), channel_id=1, source_target_pairs={{0,2},{1,3},{2,0},{3,1},{4,6},{5,7},{6,4},{7,5},{8,10},{9,11},{10,... | collective-permute-start | bytes 393224 | tf_op jit(solution)/shard_map/ppermute | solution.py:17
  351.1 4.2 %collective-permute-start.41 = (f32[8,128]{1,0:T(8,128)S(1)}, f32[8,128]{1,0:T(8,128)S(1)}, u32[]{:S(2)}, u32[]{:S(2)}) collective-permute-start(f32[8,128]{1,0:T(8,128)S(1)} %add_add_fusion), channel_id=1, source_target_pairs={{0,4},{4,0},{8,12},{12,8},{16,20},{20,16},{24,28},{28,24},{1,5},{5... | collective-permute-start | bytes 12296 | tf_op jit(solution)/shard_map/ppermute | solution.py:17
  355.2 14.3 %collective-permute-start.40 = (f32[256,128]{1,0:T(8,128)S(1)}, f32[256,128]{1,0:T(8,128)S(1)}, u32[]{:S(2)}, u32[]{:S(2)}) collective-permute-start(f32[256,128]{1,0:T(8,128)S(1)} %add.231), channel_id=1, source_target_pairs={{0,1},{1,0},{2,3},{3,2},{4,5},{5,4},{6,7},{7,6},{8,9},{9,8},{10,11... | collective-permute-start | bytes 393224 | tf_op jit(solution)/shard_map/ppermute | solution.py:17
  355.3 3.7 collective-permute-start.42
  358.9 4.5 %collective-permute-start.43 = (f32[8,128]{1,0:T(8,128)S(1)}, f32[8,128]{1,0:T(8,128)S(1)}, u32[]{:S(2)}, u32[]{:S(2)}) collective-permute-start(f32[8,128]{1,0:T(8,128)S(1)} %add.243), channel_id=1, source_target_pairs={{0,16},{4,20},{8,24},{12,28},{16,0},{20,4},{24,8},{28,12},{1,17},{... | collective-permute-start | bytes 12296 | tf_op jit(solution)/shard_map/ppermute | solution.py:17
  363.4 1.2 collective-permute-start.44
  364.6 3.6 collective-permute-start.45
  (29 other events, 258.3 us)
